TPU v7x, 32 devices: a whole 2x2x4 slice. The times are simulated.
32 devices in a mesh: groups: 2 (over x), out: 16 (over z, y, core).
Axes of the slice: x: 2, y: 2, z: 4, core: 2. Of those that a mesh axis runs over, the one named last changes fastest.
Arguments:
- tokens: bfloat16 [256, 8192], P('groups', 'out'), parts along dimension 0, may hold values from -60 to 60, as said below
- grad_hidden: bfloat16 [256, 16384], P('groups', 'out'), parts along dimension 0, may hold values from -6 to 6
- w_gate: bfloat16 [8192, 16384], P(None, 'out'), may hold values from -0.0625 to 0.0625
- w_up: bfloat16 [8192, 16384], P(None, 'out'), may hold values from -0.0625 to 0.0625
- a_factors: bfloat16 [8192, 128], replicated, may hold values from -0.0625 to 0.0625
- b_factors: bfloat16 [2, 64, 16384], P(None, None, 'out'), may hold values from -0.75 to 0.75
- magnitudes: float32 [2, 16384], P(None, 'out'), may hold values from 1 to 2
Outputs:
- hidden: bfloat16 [256, 16384], P('groups', 'out'), parts along dimension 0
- grad_tokens: bfloat16 [256, 8192], P('groups', 'out'), parts along dimension 0
- step_a: float32 [16384, 128], P(('groups', 'out')), parts along dimension 0
- step_b: float32 [4, 64, 16384], P('groups', None, 'out'), parts along dimension 0
- step_m: float32 [4, 16384], P('groups', 'out'), parts along dimension 0
There are 2 independent parts, one for each index of `groups`. A program takes and returns all parts, laid end to end along the dimension named above; an argument that names none is the same for every part. Nothing has to cross between parts.
Inputs may be any that keep to these rules, and one draw needn't show every extreme that they name: `tokens`: activations with feature scales that differ between features.
All inputs are finite; a program needn't handle non-finite values.
Results may differ from a plain program's by a relative error of at most 0.0073.
Values may be sent and summed in bfloat16 or wider, within the bound.
A program may use at most 128 MiB of HBM per device.

v0:
```python
import jax
import jax.numpy as jnp
from jax import lax
from jax.sharding import PartitionSpec as P

D = 8192
FW = 16384
R = 64


def inner_product(left_side, right_side, precision=None):
    return lax.dot_general(
        left_side,
        right_side,
        (((0,), (0,)), ((), ())),
        precision=precision,
        preferred_element_type=jnp.float32,
    )


def outer_contract(left_side, right_side, precision=None):
    return lax.dot_general(
        left_side,
        right_side,
        (((1,), (1,)), ((), ())),
        precision=precision,
        preferred_element_type=jnp.float32,
    )


def split_parts(values):
    upper = values.astype(jnp.bfloat16)
    lower = (values - upper.astype(jnp.float32)).astype(jnp.bfloat16)
    return (upper, lower)


def per_device(tokens, grad_hidden, w_gate, w_up, a_factors, b_factors, magnitudes):
    weights = (w_gate, w_up)
    rank = a_factors.shape[1] // 2
    count_tokens = tokens.shape[0]
    norms = []
    scales = []
    for which in range(2):
        weight = weights[which]
        left = a_factors[:, which * rank : (which + 1) * rank]
        right = b_factors[which]
        merged = weight.astype(jnp.float32) + jnp.dot(
            left, right, preferred_element_type=jnp.float32
        )
        squares = jnp.sum(merged * merged, axis=0)
        norm_col = jnp.sqrt(squares + 1e-06)
        norms.append(norm_col)
        scales.append(magnitudes[which] / norm_col)
    whole = lax.all_gather(tokens, "out", axis=1, tiled=True)
    base_gate = jnp.dot(whole, w_gate, preferred_element_type=jnp.float32)
    base_up = jnp.dot(whole, w_up, preferred_element_type=jnp.float32)
    low_wide = jnp.dot(whole, a_factors, preferred_element_type=jnp.float32)
    low = low_wide.astype(jnp.bfloat16)
    bases = []
    pres = []
    for which, raw in enumerate((base_gate, base_up)):
        base = raw + jnp.dot(
            low[:, which * rank : (which + 1) * rank],
            b_factors[which],
            preferred_element_type=jnp.float32,
        )
        bases.append(base)
        pres.append(base * scales[which][None, :])
    sigma = jax.nn.sigmoid(pres[0])
    hidden = (pres[0] * sigma * pres[1]).astype(jnp.bfloat16)
    cotangent = grad_hidden.astype(jnp.float32)
    dpres = (
        cotangent * pres[1] * sigma * (1.0 + pres[0] * (1.0 - sigma)),
        cotangent * pres[0] * sigma,
    )
    partial_sum = jnp.zeros((count_tokens, w_gate.shape[0]), jnp.float32)
    z_blocks = []
    grad_bs = []
    grad_ms = []
    for which in range(2):
        dscaled = (dpres[which] * scales[which][None, :]).astype(jnp.bfloat16)
        grad_ms.append(jnp.sum(dpres[which] * bases[which], axis=0) / norms[which])
        grad_bs.append(inner_product(low[:, which * rank : (which + 1) * rank], dscaled))
        z_blocks.append(outer_contract(dscaled, b_factors[which]))
        partial_sum = partial_sum + outer_contract(dscaled, weights[which])
    z_local = jnp.concatenate(z_blocks, axis=1)
    z_upper, z_lower = split_parts(z_local)
    partial_sum = (
        partial_sum + outer_contract(z_upper, a_factors) + outer_contract(z_lower, a_factors)
    )
    a_terms = inner_product(whole, z_upper) + inner_product(whole, z_lower)
    grad_a = lax.psum_scatter(a_terms, "out", scatter_dimension=0, tiled=True)
    summed_inputs = lax.psum_scatter(partial_sum, "out", scatter_dimension=1, tiled=True)
    grad_tokens = summed_inputs.astype(jnp.bfloat16)
    grad_b = jnp.stack(grad_bs)
    grad_m = jnp.stack(grad_ms)
    local_energy = jnp.sum(grad_a * grad_a) + jnp.sum(grad_b * grad_b) + jnp.sum(grad_m * grad_m)
    energy = lax.psum(local_energy, "out")
    count_all = 2 * D * R + 2 * R * FW + 2 * FW
    rms_value = jnp.sqrt(energy / count_all + 1e-06)
    return (hidden, grad_tokens, grad_a / rms_value, grad_b / rms_value, grad_m / rms_value)


def solution(mesh):
    in_specs = (
        P("groups", "out"),
        P("groups", "out"),
        P(None, "out"),
        P(None, "out"),
        P(),
        P(None, None, "out"),
        P(None, "out"),
    )
    out_specs = (
        P("groups", "out"),
        P("groups", "out"),
        P(("groups", "out"), None),
        P("groups", None, "out"),
        P("groups", "out"),
    )
    return jax.shard_map(
        per_device, mesh=mesh, in_specs=in_specs, out_specs=out_specs, check_vma=False
    )
```

profile of v0, /device:TPU:0, one launch (start us, length us, event | category | flops | bytes accessed | tf_op | source)
XLA Modules:
  0.0 230.4 jit_solution(6841040627441248489)
XLA Ops:
  8.0 8.9 %multiply_reduce_fusion.1 = f32[1024]{0:T(1024)S(1)} fusion(bf16[8192,1024]{1,0:T(8,128)(2,1)} %param.9, bf16[8192,128]{1,0:T(8,128)(2,1)} %param.11, bf16[2,64,1024]{2,1,0:T(8,128)(2,1)} %param.12), kind=kOutput, calls=%fused_computation.1 | convolution fusion | flops 1107295232 | bytes 19009536 | tf_op jit(solution)/shard_map/dot_general | solution.py:47
  16.9 2.9 %copy-done = bf16[8192,1024]{1,0:T(8,128)(2,1)S(1)} copy-done((bf16[8192,1024]{1,0:T(8,128)(2,1)S(1)}, bf16[8192,1024]{1,0:T(8,128)(2,1)}, u32[]{:S(2)}) %copy-start) | copy-done | bytes 16777240
  19.8 5.5 %multiply_reduce_fusion = f32[1024]{0:T(1024)S(1)} fusion(bf16[8192,1024]{1,0:T(8,128)(2,1)S(1)} %copy-done, bf16[8192,128]{1,0:T(8,128)(2,1)S(1)} %copy-done.2, bf16[2,64,1024]{2,1,0:T(8,128)(2,1)S(1)} %copy-done.3), kind=kOutput, calls=%fused_computation | convolution fusion | flops 1107295232 | bytes 19009536 | tf_op jit(solution)/shard_map/dot_general | solution.py:47
  25.4 28.7 %all-gather.2.cloned.1.call-done = bf16[128,8192]{1,0:T(8,128)(2,1)} async-done(((bf16[128,512]{1,0:T(8,128)(2,1)}), bf16[128,8192]{1,0:T(8,128)(2,1)}) %all-gather.2.cloned.1.call-update) | async-done | bytes 2097168 | tf_op jit(solution)/shard_map/all_gather | solution.py:54
  54.1 2.7 %convolution_convert_fusion = bf16[128,128]{0,1:T(8,128)(2,1)S(1)} fusion(bf16[128,8192]{1,0:T(8,128)(2,1)} %all-gather.2.cloned.1.call-done, bf16[8192,128]{1,0:T(8,128)(2,1)S(1)} %copy-done.2), kind=kOutput, calls=%fused_computation.13 | convolution fusion | flops 268451840 | bytes 4227072 | tf_op jit(solution)/shard_map/dot_general | solution.py:57
  56.8 8.9 %fusion.32 = f32[128,1024]{1,0:T(8,128)S(1)} fusion(bf16[128,8192]{1,0:T(8,128)(2,1)} %all-gather.2.cloned.1.call-done, bf16[8192,1024]{1,0:T(8,128)(2,1)} %param.10), kind=kOutput, calls=%fused_computation.62 | convolution fusion | flops 2147483648 | bytes 19398656 | tf_op jit(solution)/shard_map/dot_general | solution.py:56
  66.0 0.8 slice-done.3
  67.4 2.4 %fusion.31 = f32[128,1024]{1,0:T(8,128)S(1)} fusion(bf16[128,8192]{1,0:T(8,128)(2,1)S(1)} %copy-done.1, bf16[8192,1024]{1,0:T(8,128)(2,1)S(1)} %bitcast.47), kind=kOutput, calls=%fused_computation.61 | convolution fusion | flops 2147483648 | bytes 19398656 | tf_op jit(solution)/shard_map/dot_general | solution.py:55
  69.9 1.3 multiply_reduce_fusion.3
  71.6 0.7 fusion.26
  72.3 2.6 %fusion = f32[8192,128]{0,1:T(8,128)} fusion(f32[128,8192]{1,0:T(8,128)S(1)} %fusion.26, bf16[128,8192]{1,0:T(8,128)(2,1)S(1)} %copy-done.1, f32[128,64]{0,1:T(8,128)S(1)} %fusion.7, f32[128,64]{0,1:T(8,128)S(1)} %fusion.11), kind=kOutput, calls=%fused_computation.3 | convolution fusion | flops 269565952 | bytes 10551296 | tf_op jit(solution)/shard_map/dot_general | solution.py:12
  75.3 13.5 %fusion.33 = f32[128,8192]{1,0:T(8,128)} fusion(bf16[128,1024]{1,0:T(8,128)(2,1)S(1)} %get-tuple-element.12, bf16[8192,1024]{1,0:T(8,128)(2,1)} %param.9), kind=kOutput, calls=%fused_computation.63 | convolution fusion | flops 2147483648 | bytes 21233664 | tf_op jit(solution)/shard_map/dot_general | solution.py:22
  88.8 15.3 %convolution_add_fusion.3 = f32[128,8192]{1,0:T(8,128)} fusion(f32[128,8192]{1,0:T(8,128)} %fusion.33, bf16[128,1024]{1,0:T(8,128)(2,1)S(1)} %get-tuple-element.14, bf16[8192,1024]{1,0:T(8,128)(2,1)} %param.10), kind=kOutput, calls=%fused_computation.6 | convolution fusion | flops 2148532224 | bytes 25427968 | tf_op jit(solution)/shard_map/dot_general | solution.py:22
  104.1 3.0 %convolution_add_fusion.2 = f32[128,8192]{1,0:T(8,128)S(1)} fusion(f32[128,8192]{1,0:T(8,128)} %convolution_add_fusion.3, bf16[8192,128]{1,0:T(8,128)(2,1)S(1)} %copy-done.2, f32[128,64]{0,1:T(8,128)S(1)} %fusion.7, f32[128,64]{0,1:T(8,128)S(1)} %fusion.11), kind=kOutput, calls=%fused_computation.5 | convolution fusion | flops 269549568 | bytes 10551296 | tf_op jit(solution)/shard_map/dot_general | solution.py:22
  107.1 2.8 %convolution_add_fusion.1 = f32[128,8192]{1,0:T(8,128)} fusion(f32[128,8192]{1,0:T(8,128)S(1)} %convolution_add_fusion.2, bf16[8192,128]{1,0:T(8,128)(2,1)S(1)} %copy-done.2, f32[128,64]{0,1:T(8,128)S(1)} %fusion.7, f32[128,64]{0,1:T(8,128)S(1)} %fusion.11), kind=kOutput, calls=%fused_computation.4 | convolution fusion | flops 269565952 | bytes 10551296 | tf_op jit(solution)/shard_map/dot_general | solution.py:22
  110.9 0.7 multiply_reduce_fusion.4
  111.6 34.9 %reduce-scatter.5.cloned.1.call-done = f32[512,128]{0,1:T(8,128)} async-done(((f32[8192,128]{0,1:T(8,128)}), f32[512,128]{0,1:T(8,128)}) %reduce-scatter.5.cloned.1.call-update) | async-done | bytes 262160 | tf_op jit(solution)/shard_map/reduce_scatter | solution.py:92
  146.5 1.6 multiply_reduce_fusion.5
  150.1 30.5 %psum.7 = f32[]{:T(128)} all-reduce(f32[]{:T(128)S(6)} %add.92), channel_id=1, replica_groups=mesh['groups'=2,'out'=16] {'out'}, use_global_device_ids=true, to_apply=%region_9.0 | all-reduce | flops 1 | bytes 8 | tf_op jit(solution)/shard_map/psum | solution.py:98
  181.3 1.0 broadcast_divide_fusion
  182.3 0.8 copy.12
  183.8 0.9 fusion.6
  184.6 37.7 %reduce-scatter.3.cloned.1.call-done = f32[128,512]{1,0:T(8,128)} async-done(((f32[128,8192]{1,0:T(8,128)}), f32[128,512]{1,0:T(8,128)}) %reduce-scatter.3.cloned.1.call-update) | async-done | bytes 262160 | tf_op jit(solution)/shard_map/reduce_scatter | solution.py:93
  222.3 1.6 convert_element_type.43
  (37 shorter events, 3.9 us)
Async XLA Ops:
  7.2 46.9 %all-gather.2.cloned.1.call-start = ((), (), s32[]{:S(2)}) async-start(), calls=%async_computation.2 | async-start | bytes 2228224 | tf_op jit(solution)/shard_map/all_gather | solution.py:54
  7.9 9.0 %copy-start.2 = (bf16[8192,128]{1,0:T(8,128)(2,1)S(1)}, bf16[8192,128]{1,0:T(8,128)(2,1)}, u32[]{:S(2)}) copy-start(bf16[8192,128]{1,0:T(8,128)(2,1)} %param.11) | copy-start | bytes 6291460
  7.9 9.0 %copy-start.3 = (bf16[2,64,1024]{2,1,0:T(8,128)(2,1)S(1)}, bf16[2,64,1024]{2,1,0:T(8,128)(2,1)}, u32[]{:S(2)}) copy-start(bf16[2,64,1024]{2,1,0:T(8,128)(2,1)} %param.12) | copy-start | bytes 786436
  7.9 138.6 %reduce-scatter.5.cloned.1.call-start = ((), (), s32[]{:S(2)}) async-start(), calls=%async_computation.4 | async-start | bytes 4456448 | tf_op jit(solution)/shard_map/reduce_scatter | solution.py:92
  8.0 11.9 %copy-start = (bf16[8192,1024]{1,0:T(8,128)(2,1)S(1)}, bf16[8192,1024]{1,0:T(8,128)(2,1)}, u32[]{:S(2)}) copy-start(bf16[8192,1024]{1,0:T(8,128)(2,1)} %param.10) | copy-start | bytes 50331652
  19.8 5.6 %copy-start.4 = (f32[2,1024]{1,0:T(2,128)S(1)}, f32[2,1024]{1,0:T(2,128)}, u32[]{:S(2)}) copy-start(f32[2,1024]{1,0:T(2,128)} %param.13) | copy-start | bytes 24580
  54.1 11.9 %slice-start = ((s8[16777216]{0:T(1024)(128)(4,1)}), s8[4194304]{0:T(1024)(128)(4,1)S(1)}, s32[]{:S(2)}) async-start(s8[16777216]{0:T(1024)(128)(4,1)} %bitcast.46), calls=%async_computation.5 | async-start | bytes 8388608
  56.8 9.2 %slice-start.1 = ((s8[16777216]{0:T(1024)(128)(4,1)}), s8[4194304]{0:T(1024)(128)(4,1)S(1)}, s32[]{:S(2)}) async-start(s8[16777216]{0:T(1024)(128)(4,1)} %bitcast.46), calls=%async_computation.6 | async-start | bytes 8388608
  56.8 9.2 %slice-start.2 = ((s8[16777216]{0:T(1024)(128)(4,1)}), s8[4194304]{0:T(1024)(128)(4,1)S(1)}, s32[]{:S(2)}) async-start(s8[16777216]{0:T(1024)(128)(4,1)} %bitcast.46), calls=%async_computation.7 | async-start | bytes 8388608
  56.8 10.0 %slice-start.3 = ((s8[16777216]{0:T(1024)(128)(4,1)}), s8[4194304]{0:T(1024)(128)(4,1)S(1)}, s32[]{:S(2)}) async-start(s8[16777216]{0:T(1024)(128)(4,1)} %bitcast.46), calls=%async_computation.8 | async-start | bytes 8388608
  56.8 10.6 %copy-start.1 = (bf16[128,8192]{1,0:T(8,128)(2,1)S(1)}, bf16[128,8192]{1,0:T(8,128)(2,1)}, u32[]{:S(2)}) copy-start(bf16[128,8192]{1,0:T(8,128)(2,1)} %all-gather.2.cloned.1.call-done) | copy-start | bytes 6291460
  67.4 2.5 %copy-start.5 = (bf16[128,1024]{1,0:T(8,128)(2,1)S(1)}, bf16[128,1024]{1,0:T(8,128)(2,1)}, u32[]{:S(2)}) copy-start(bf16[128,1024]{1,0:T(8,128)(2,1)} %param.8) | copy-start | bytes 786436
  75.0 147.3 %reduce-scatter.3.cloned.1.call-start = ((), (), s32[]{:S(2)}) async-start(), calls=%async_computation.3 | async-start | bytes 4456448 | tf_op jit(solution)/shard_map/reduce_scatter | solution.py:93
Sparse Core Ops, SparseCore 0:
  10.2 43.8 all-gather.1
  75.1 71.3 reduce-scatter.4
  150.9 71.3 reduce-scatter.2
where the time goes:
time: 231 us; the launch traced here: 230 us
  waiting for transfers between devices  102 us (44%)
  matrix products  68.7 us (30%)
  blocking collectives  30.5 us (13%)
  between operations  16.6 us (7%)
  other arithmetic  7.07 us (3%)
  local copies, waits for them, and re-layouts  5.15 us (2%)
    reduce_scatter x1, waiting for transfers between devices, per_device(): lax.psum_scatter(partial_sum, 'out', scatter_dimension=1, tiled=True)  37.7 us
    dot_general x6, matrix products, outer_contract(): lax.dot_general(left_side, right_side, (((1,), (1,)), ((), ())), precisio...  35 us
    reduce_scatter x1, waiting for transfers between devices, per_device(): grad_a = lax.psum_scatter(a_terms, 'out', scatter_dimension=0, tiled=True)  34.9 us
    psum x1, blocking collectives, per_device(): energy = lax.psum(local_energy, 'out')  30.5 us
    all_gather x1, waiting for transfers between devices, per_device(): whole = lax.all_gather(tokens, 'out', axis=1, tiled=True)  28.7 us
    dot_general x2, matrix products, per_device(): jnp.dot(left, right, preferred_element_type=jnp.float32)  14.5 us
    dot_general x1, matrix products, per_device(): base_up = jnp.dot(whole, w_up, preferred_element_type=jnp.float32)  8.88 us
    unnamed x21, local copies, waits for them, and re-layouts  5.15 us
  transfers between devices with their start and end apart: 3, of which 3 were waited for; matrix products, arithmetic and copies ran while one was open for 24% of the time, Pallas kernels for 0%

commit v1 on v0

--- a/solution.py
+++ b/solution.py
@@ -84,18 +84,19 @@
         z_blocks.append(outer_contract(dscaled, b_factors[which]))
         partial_sum = partial_sum + outer_contract(dscaled, weights[which])
     z_local = jnp.concatenate(z_blocks, axis=1)
-    z_upper, z_lower = split_parts(z_local)
-    partial_sum = (
-        partial_sum + outer_contract(z_upper, a_factors) + outer_contract(z_lower, a_factors)
-    )
-    a_terms = inner_product(whole, z_upper) + inner_product(whole, z_lower)
-    grad_a = lax.psum_scatter(a_terms, "out", scatter_dimension=0, tiled=True)
-    summed_inputs = lax.psum_scatter(partial_sum, "out", scatter_dimension=1, tiled=True)
-    grad_tokens = summed_inputs.astype(jnp.bfloat16)
     grad_b = jnp.stack(grad_bs)
     grad_m = jnp.stack(grad_ms)
-    local_energy = jnp.sum(grad_a * grad_a) + jnp.sum(grad_b * grad_b) + jnp.sum(grad_m * grad_m)
-    energy = lax.psum(local_energy, "out")
+    summed_inputs = lax.psum_scatter(partial_sum, "out", scatter_dimension=1, tiled=True)
+    local_energy = jnp.sum(grad_b * grad_b) + jnp.sum(grad_m * grad_m)
+    z_all, small_energy = lax.psum((z_local, local_energy), "out")
+    z_upper, z_lower = split_parts(z_all)
+    full_a = inner_product(whole, z_upper) + inner_product(whole, z_lower)
+    grad_a = inner_product(tokens, z_upper) + inner_product(tokens, z_lower)
+    mine = tokens.shape[1]
+    a_mine = lax.dynamic_slice_in_dim(a_factors, lax.axis_index("out") * mine, mine, 0)
+    adapter = outer_contract(z_upper, a_mine) + outer_contract(z_lower, a_mine)
+    grad_tokens = (summed_inputs + adapter).astype(jnp.bfloat16)
+    energy = small_energy + jnp.sum(full_a * full_a)
     count_all = 2 * D * R + 2 * R * FW + 2 * FW
     rms_value = jnp.sqrt(energy / count_all + 1e-06)
     return (hidden, grad_tokens, grad_a / rms_value, grad_b / rms_value, grad_m / rms_value)

time: 231 us -> 257 us (1.11)
  waiting for transfers between devices: 102 us -> 133 us
  matrix products: 68.7 us -> 64.5 us
  other arithmetic: 7.07 us -> 4.41 us
    reduce_scatter x1 -> x0, waiting for transfers between devices: 34.9 us -> none  [per_device(): grad_a = lax.psum_scatter(a_terms, 'out', scatter_dimension=0, tiled=True)]
    psum x0 -> x1, waiting for transfers between devices: none -> 33.7 us  [per_device(): z_all, small_energy = lax.psum((z_local, local_energy), 'out')]
    reduce_scatter x1, waiting for transfers between devices: 37.7 us -> 69.9 us  [per_device(): lax.psum_scatter(partial_sum, 'out', scatter_dimension=1, tiled=True)]
    dot_general x6, matrix products: 35 us -> 31.2 us  [outer_contract(): lax.dot_general(left_side, right_side, (((1,), (1,)), ((), ())), precisio...]
    unnamed x21 -> x23, local copies, waits for them, and re-layouts: 5.15 us -> 5.16 us
  transfers between devices with their start and end apart: 3 -> 3, of which waited for: 3 -> 3; matrix products, arithmetic and copies ran while one was open for 24% -> 15% of each run, Pallas kernels for 0% -> 0%
where the time goes in v1:
time: 257 us; the launch traced here: 256 us
  waiting for transfers between devices  133 us (52%)
  matrix products  64.5 us (25%)
  blocking collectives  32.1 us (12%)
  between operations  16.7 us (6%)
  local copies, waits for them, and re-layouts  5.16 us (2%)
  other arithmetic  4.41 us (2%)
    reduce_scatter x1, waiting for transfers between devices, per_device(): lax.psum_scatter(partial_sum, 'out', scatter_dimension=1, tiled=True)  69.9 us
    psum x1, waiting for transfers between devices, per_device(): z_all, small_energy = lax.psum((z_local, local_energy), 'out')  33.7 us
    psum x1, blocking collectives, per_device(): z_all, small_energy = lax.psum((z_local, local_energy), 'out')  32.1 us
    dot_general x6, matrix products, outer_contract(): lax.dot_general(left_side, right_side, (((1,), (1,)), ((), ())), precisio...  31.2 us
    all_gather x1, waiting for transfers between devices, per_device(): whole = lax.all_gather(tokens, 'out', axis=1, tiled=True)  28.7 us
    dot_general x2, matrix products, per_device(): jnp.dot(left, right, preferred_element_type=jnp.float32)  14.4 us
    dot_general x1, matrix products, per_device(): base_up = jnp.dot(whole, w_up, preferred_element_type=jnp.float32)  8.88 us
    unnamed x23, local copies, waits for them, and re-layouts  5.16 us
  transfers between devices with their start and end apart: 3, of which 3 were waited for; matrix products, arithmetic and copies ran while one was open for 15% of the time, Pallas kernels for 0%

profile of v1, /device:TPU:0, one launch (start us, length us, event | category | flops | bytes accessed | tf_op | source)
XLA Modules:
  0.0 256.2 jit_solution(1929650667966069490)
XLA Ops:
  7.2 0.7 all-gather.2.cloned.1.call-update
  8.0 8.9 %multiply_reduce_fusion.1 = f32[1024]{0:T(1024)S(1)} fusion(bf16[8192,1024]{1,0:T(8,128)(2,1)} %param.9, bf16[8192,128]{1,0:T(8,128)(2,1)} %param.11, bf16[2,64,1024]{2,1,0:T(8,128)(2,1)} %param.12), kind=kOutput, calls=%fused_computation.1 | convolution fusion | flops 1107295232 | bytes 19009536 | tf_op jit(solution)/shard_map/dot_general | solution.py:47
  16.9 2.9 %copy-done = bf16[8192,1024]{1,0:T(8,128)(2,1)S(1)} copy-done((bf16[8192,1024]{1,0:T(8,128)(2,1)S(1)}, bf16[8192,1024]{1,0:T(8,128)(2,1)}, u32[]{:S(2)}) %copy-start) | copy-done | bytes 16777240
  19.8 5.5 %multiply_reduce_fusion = f32[1024]{0:T(1024)S(1)} fusion(bf16[8192,1024]{1,0:T(8,128)(2,1)S(1)} %copy-done, bf16[8192,128]{1,0:T(8,128)(2,1)S(1)} %copy-done.2, bf16[2,64,1024]{2,1,0:T(8,128)(2,1)S(1)} %copy-done.3), kind=kOutput, calls=%fused_computation | convolution fusion | flops 1107295232 | bytes 19009536 | tf_op jit(solution)/shard_map/dot_general | solution.py:47
  25.4 28.7 %all-gather.2.cloned.1.call-done = bf16[128,8192]{1,0:T(8,128)(2,1)} async-done(((bf16[128,512]{1,0:T(8,128)(2,1)}), bf16[128,8192]{1,0:T(8,128)(2,1)}) %all-gather.2.cloned.1.call-update) | async-done | bytes 2097168 | tf_op jit(solution)/shard_map/all_gather | solution.py:54
  54.1 2.7 %convolution_convert_fusion = bf16[128,128]{0,1:T(8,128)(2,1)S(1)} fusion(bf16[128,8192]{1,0:T(8,128)(2,1)} %all-gather.2.cloned.1.call-done, bf16[8192,128]{1,0:T(8,128)(2,1)S(1)} %copy-done.2), kind=kOutput, calls=%fused_computation.18 | convolution fusion | flops 268451840 | bytes 4227072 | tf_op jit(solution)/shard_map/dot_general | solution.py:57
  56.8 8.9 %fusion.36 = f32[128,1024]{1,0:T(8,128)S(1)} fusion(bf16[128,8192]{1,0:T(8,128)(2,1)} %all-gather.2.cloned.1.call-done, bf16[8192,1024]{1,0:T(8,128)(2,1)} %param.10), kind=kOutput, calls=%fused_computation.66 | convolution fusion | flops 2147483648 | bytes 19398656 | tf_op jit(solution)/shard_map/dot_general | solution.py:56
  66.0 0.8 slice-done.3
  67.4 2.5 fusion.35
  69.9 1.3 multiply_reduce_fusion.3
  71.4 13.2 %fusion.37 = f32[128,8192]{1,0:T(8,128)} fusion(bf16[128,1024]{1,0:T(8,128)(2,1)S(1)} %get-tuple-element.14, bf16[8192,1024]{1,0:T(8,128)(2,1)} %param.9), kind=kOutput, calls=%fused_computation.67 | convolution fusion | flops 2147483648 | bytes 21233664 | tf_op jit(solution)/shard_map/dot_general | solution.py:22
  84.9 0.6 pad_maximum_fusion.1
  85.8 14.5 %convolution_add_fusion.1 = f32[128,8192]{1,0:T(8,128)} fusion(f32[128,8192]{1,0:T(8,128)} %fusion.37, bf16[128,1024]{1,0:T(8,128)(2,1)S(1)} %get-tuple-element.16, bf16[8192,1024]{1,0:T(8,128)(2,1)} %param.10), kind=kOutput, calls=%fused_computation.4 | convolution fusion | flops 2148532224 | bytes 25427968 | tf_op jit(solution)/shard_map/dot_general | solution.py:22
  101.4 0.7 multiply_reduce_fusion.4
  103.4 32.1 %psum.15 = f32[]{:T(128)} all-reduce(f32[]{:T(128)S(6)} %add.96), channel_id=1, replica_groups=mesh['groups'=2,'out'=16] {'out'}, use_global_device_ids=true, to_apply=%region_8.0 | all-reduce | flops 1 | bytes 8 | tf_op jit(solution)/shard_map/psum | solution.py:91
  135.5 33.7 %all-reduce.2.cloned.1.call-done = f32[128,128]{0,1:T(8,128)} async-done(((f32[128,128]{0,1:T(8,128)}), f32[128,128]{0,1:T(8,128)}) %all-reduce.2.cloned.1.call-update) | async-done | bytes 65552 | tf_op jit(solution)/shard_map/psum | solution.py:91
  169.2 0.9 subtract_convert_fusion
  170.1 0.7 fusion.39
  170.8 1.9 fusion.3
  174.5 0.8 copy.12
  175.9 0.9 fusion.11
  176.8 1.1 fusion.21
  177.9 69.9 %reduce-scatter.2.cloned.1.call-done = f32[128,512]{1,0:T(8,128)} async-done(((f32[128,8192]{1,0:T(8,128)}), f32[128,512]{1,0:T(8,128)}) %reduce-scatter.2.cloned.1.call-update) | async-done | bytes 262160 | tf_op jit(solution)/shard_map/reduce_scatter | solution.py:89
  247.8 1.9 fusion.7
  (40 shorter events, 3.6 us)
Async XLA Ops:
  7.2 46.9 %all-gather.2.cloned.1.call-start = ((), (), s32[]{:S(2)}) async-start(), calls=%async_computation.1 | async-start | bytes 2228224 | tf_op jit(solution)/shard_map/all_gather | solution.py:54
  7.9 9.0 %copy-start.2 = (bf16[8192,128]{1,0:T(8,128)(2,1)S(1)}, bf16[8192,128]{1,0:T(8,128)(2,1)}, u32[]{:S(2)}) copy-start(bf16[8192,128]{1,0:T(8,128)(2,1)} %param.11) | copy-start | bytes 6291460
  7.9 9.0 %copy-start.3 = (bf16[2,64,1024]{2,1,0:T(8,128)(2,1)S(1)}, bf16[2,64,1024]{2,1,0:T(8,128)(2,1)}, u32[]{:S(2)}) copy-start(bf16[2,64,1024]{2,1,0:T(8,128)(2,1)} %param.12) | copy-start | bytes 786436
  7.9 161.3 %all-reduce.2.cloned.1.call-start = ((), (), s32[]{:S(2)}) async-start(), calls=%async_computation.3 | async-start | bytes 131072 | tf_op jit(solution)/shard_map/psum | solution.py:91
  8.0 11.9 %copy-start = (bf16[8192,1024]{1,0:T(8,128)(2,1)S(1)}, bf16[8192,1024]{1,0:T(8,128)(2,1)}, u32[]{:S(2)}) copy-start(bf16[8192,1024]{1,0:T(8,128)(2,1)} %param.10) | copy-start | bytes 50331652
  19.8 5.5 %copy-start.5 = (f32[2,1024]{1,0:T(2,128)S(1)}, f32[2,1024]{1,0:T(2,128)}, u32[]{:S(2)}) copy-start(f32[2,1024]{1,0:T(2,128)} %param.13) | copy-start | bytes 24580
  54.1 11.9 %slice-start = ((s8[16777216]{0:T(1024)(128)(4,1)}), s8[4194304]{0:T(1024)(128)(4,1)S(1)}, s32[]{:S(2)}) async-start(s8[16777216]{0:T(1024)(128)(4,1)} %bitcast.52), calls=%async_computation.4 | async-start | bytes 8388608
  56.8 9.2 %slice-start.1 = ((s8[16777216]{0:T(1024)(128)(4,1)}), s8[4194304]{0:T(1024)(128)(4,1)S(1)}, s32[]{:S(2)}) async-start(s8[16777216]{0:T(1024)(128)(4,1)} %bitcast.52), calls=%async_computation.5 | async-start | bytes 8388608
  56.8 9.2 %slice-start.2 = ((s8[16777216]{0:T(1024)(128)(4,1)}), s8[4194304]{0:T(1024)(128)(4,1)S(1)}, s32[]{:S(2)}) async-start(s8[16777216]{0:T(1024)(128)(4,1)} %bitcast.52), calls=%async_computation.6 | async-start | bytes 8388608
  56.8 10.0 %slice-start.3 = ((s8[16777216]{0:T(1024)(128)(4,1)}), s8[4194304]{0:T(1024)(128)(4,1)S(1)}, s32[]{:S(2)}) async-start(s8[16777216]{0:T(1024)(128)(4,1)} %bitcast.52), calls=%async_computation.7 | async-start | bytes 8388608
  56.8 10.6 %copy-start.1 = (bf16[128,8192]{1,0:T(8,128)(2,1)S(1)}, bf16[128,8192]{1,0:T(8,128)(2,1)}, u32[]{:S(2)}) copy-start(bf16[128,8192]{1,0:T(8,128)(2,1)} %all-gather.2.cloned.1.call-done) | copy-start | bytes 6291460
  67.4 2.5 copy-start.6
  85.6 162.2 %reduce-scatter.2.cloned.1.call-start = ((), (), s32[]{:S(2)}) async-start(), calls=%async_computation.2 | async-start | bytes 4456448 | tf_op jit(solution)/shard_map/reduce_scatter | solution.py:89
  170.8 3.3 %copy-start.4 = (bf16[128,512]{1,0:T(8,128)(2,1)S(1)}, bf16[128,512]{1,0:T(8,128)(2,1)}, u32[]{:S(2)}) copy-start(bf16[128,512]{1,0:T(8,128)(2,1)} %param.7) | copy-start | bytes 393220
Sparse Core Ops, SparseCore 0:
  10.2 43.8 all-gather.1
  85.7 83.4 all-reduce.1
  173.6 74.2 reduce-scatter.1

commit v2 on v0

v2 whole, which is shorter than its diff:
```python
import functools

import jax
import jax.numpy as jnp
from jax import lax
from jax.experimental import pallas as pl
from jax.experimental.pallas import tpu as pltpu
from jax.sharding import PartitionSpec as P

F32 = jnp.float32
BF16 = jnp.bfloat16


def mm(left, right):
    return lax.dot_general(left, right, (((1,), (0,)), ((), ())), preferred_element_type=F32)


def mm_t(left, right):
    return lax.dot_general(left, right, (((1,), (1,)), ((), ())), preferred_element_type=F32)


def split_parts(values):
    upper = values.astype(BF16)
    lower = (values - upper.astype(F32)).astype(BF16)
    return upper, lower


def fold_rows(values):
    rows, cols = values.shape
    return jnp.sum(values.reshape(rows // 8, 8, cols), axis=0)


def kernel(
    n, tok, gh, wg, wu, a, b, mag,
    hidden, gtok, step_a, step_b, step_m,
    wbuf, gat, bpad, sq, base, low, ds, own, sc, rc, sm, rm, sh, rh, z0, zc, z1, zm, zh,
    w_sem, ga_send, ga_recv, c_send, c_recv, m_send, m_recv, h_send, h_recv, z_send, z_recv,
):
    nh = n // 4
    width = a.shape[1]
    rank = width // 2
    depth = a.shape[0]
    block = depth // n
    cols = gh.shape[1]
    tokens = tok.shape[0]
    me = lax.axis_index("out")
    core = lax.rem(me, 2)
    mid = lax.rem(me // 2, 2)
    hi = me // 4

    def place(h, m, c):
        return (h * 2 + m) * 2 + c

    core_peer = place(hi, mid, 1 - core)
    mid_peer = place(hi, 1 - mid, core)

    def hi_after(k):
        return lax.rem(hi + 1 + k, nh)

    def hi_before(k):
        return lax.rem(hi + 2 * nh - 1 - k, nh)

    def remote(src, dst, send, recv, target):
        return pltpu.make_async_remote_copy(
            src_ref=src, dst_ref=dst, send_sem=send, recv_sem=recv,
            device_id={"out": target}, device_id_type=pl.DeviceIdType.MESH,
        )

    def rows_of(j):
        return pl.ds(pl.multiple_of(j * block, block), block)

    def weight_copy(which, j):
        source = wg if which == 0 else wu
        return pltpu.make_async_copy(
            source.at[rows_of(j), :], wbuf.at[which, rows_of(j), :], w_sem.at[which, j]
        )

    @pl.loop(0, n)
    def _(j):
        weight_copy(0, j).start()
        weight_copy(1, j).start()

    barrier = pltpu.get_barrier_semaphore()
    peers = [core_peer, mid_peer] + [place(hi_after(k), mid, core) for k in range(nh - 1)]
    for peer in peers:
        pl.semaphore_signal(
            barrier, inc=1, device_id={"out": peer}, device_id_type=pl.DeviceIdType.MESH
        )
    pl.semaphore_wait(barrier, len(peers))

    pending = []
    count = [0]

    def gather_send(src, origin, target):
        copy = remote(src, gat.at[origin], ga_send.at[count[0]], ga_recv.at[origin], target)
        count[0] += 1
        copy.start()
        pending.append(copy)

    def gather_wait(origin):
        remote(gat.at[origin], gat.at[origin], ga_send.at[0], ga_recv.at[origin], core_peer).wait_recv()

    gather_send(tok, me, mid_peer)
    for k in range(nh - 1):
        gather_send(tok, me, place(hi_after(k), mid, core))
    gather_send(tok, me, core_peer)
    gat[me] = tok[...]

    bpad[...] = jnp.zeros_like(bpad)
    bpad[0, :rank, :] = b[0]
    bpad[1, rank:, :] = b[1]
    sq[...] = jnp.zeros_like(sq)

    events = {}

    def from_hi(k):
        origin = place(hi_before(k), mid, core)
        gather_wait(origin)
        gather_send(gat.at[origin], origin, mid_peer)
        gather_send(gat.at[origin], origin, core_peer)

    def from_mid(k):
        origin = place(hi if k == 0 else hi_before(k - 1), 1 - mid, core)
        gather_wait(origin)
        gather_send(gat.at[origin], origin, core_peer)

    for k in range(nh - 1):
        events.setdefault(n // 4 + (k * n) // (2 * nh), []).append(functools.partial(from_hi, k))
    for k in range(nh):
        events.setdefault(min(n, n * 5 // 16 + (k * n * 3) // (4 * nh)), []).append(
            functools.partial(from_mid, k)
        )

    part = min(128, block)

    def norm_step(j):
        for which in range(2):
            weight_copy(which, j).wait()

        @pl.loop(0, block // part)
        def _(i):
            rows = pl.ds(pl.multiple_of(j * block + i * part, part), part)
            left = a[rows, :]
            for which in range(2):
                merged = wbuf[which, rows, :].astype(F32) + mm(left, bpad[which])
                sq[which] += fold_rows(merged * merged)

    marks = sorted(set([0, n] + list(events)))
    for start, end in zip(marks, marks[1:] + [None]):
        for event in events.get(start, []):
            event()
        if end is not None:
            pl.loop(start, end)(norm_step)

    base[...] = jnp.zeros_like(base)
    low[...] = jnp.zeros_like(low)

    def forward(j):
        x = gat[j]
        for which in range(2):
            base[which] += mm(x, wbuf[which, rows_of(j), :])
        low[...] += mm(x, a[rows_of(j), :])

    @pl.loop(0, n // 2)
    def _(q):
        forward(2 * q + core)

    @pl.loop(0, n // 2)
    def _(q):
        origin = 2 * q + 1 - core
        gather_wait(origin)
        forward(origin)

    low_bf = low[...].astype(BF16)
    low_t = jnp.transpose(low[...]).astype(BF16)
    piece = min(256, cols)
    for c0 in range(0, cols, piece):
        cut = slice(c0, c0 + piece)
        norms, scales, bases, pres = [], [], [], []
        for which in range(2):
            norm = jnp.sqrt(jnp.sum(sq[which, :, cut], axis=0, keepdims=True) + 1e-06)
            norms.append(norm)
            scales.append(mag[which : which + 1, cut] / norm)
            bases.append(base[which, :, cut] + mm(low_bf, bpad[which, :, cut]))
            pres.append(bases[which] * scales[which])
        sigma = 1.0 / (1.0 + jnp.exp(-pres[0]))
        hidden[:, cut] = (pres[0] * sigma * pres[1]).astype(BF16)
        cot = gh[:, cut].astype(F32)
        dpres = (
            cot * pres[1] * sigma * (1.0 + pres[0] * (1.0 - sigma)),
            cot * pres[0] * sigma,
        )
        for which in range(2):
            dscaled = (dpres[which] * scales[which]).astype(BF16)
            ds[which, :, cut] = dscaled
            step_m[which : which + 1, cut] = (
                jnp.sum(dpres[which] * bases[which], axis=0, keepdims=True) / norms[which]
            )
            step_b[which, :, cut] = mm(low_t[which * rank : (which + 1) * rank, :], dscaled)

    z0[:tokens, :] = mm_t(ds[0], bpad[0]) + mm_t(ds[1], bpad[1])
    lanes = jnp.zeros((8, width), F32)
    for c0 in range(0, cols, width):
        for which in range(2):
            value = step_b[which, :, c0 : c0 + width]
            lanes += fold_rows(value * value)
            line = step_m[which : which + 1, c0 : c0 + width]
            lanes += jnp.where(
                lax.broadcasted_iota(jnp.int32, (8, width), 0) == 0, line * line, 0.0
            )
    z0[tokens:, :] = lanes

    def start(copy):
        copy.start()
        pending.append(copy)
        return copy

    z_core = start(remote(z0, zc, z_send.at[0], z_recv.at[0], core_peer))

    def partial(j):
        return mm_t(ds[0], wbuf[0, rows_of(j), :]) + mm_t(ds[1], wbuf[1, rows_of(j), :])

    core_copies, mid_copies, hi_copies, z_hi = [], [], [], []
    z_mid = []

    def core_stage(i):
        core_copies[i].wait_recv()
        total = own[i] + rc[i].astype(F32)
        if i < nh:
            sm[i] = total.astype(BF16)
            mid_copies.append(start(remote(sm.at[i], rm.at[i], m_send.at[i], m_recv.at[i], mid_peer)))
        else:
            own[i] = total

    def mid_stage(k):
        mid_copies[k].wait_recv()
        total = own[nh + k] + rm[k].astype(F32)
        if k < nh - 1:
            sh[k] = total.astype(BF16)
            hi_copies.append(
                start(
                    remote(
                        sh.at[k], rh.at[k], h_send.at[k], h_recv.at[k],
                        place(hi_after(k), mid, core),
                    )
                )
            )
        else:
            own[nh + k] = total

    for i in range(2 * nh):
        m = 1 - mid if i < nh else mid
        h = hi_after(i % nh)
        sc[i] = partial(place(h, m, 1 - core)).astype(BF16)
        core_copies.append(start(remote(sc.at[i], rc.at[i], c_send.at[i], c_recv.at[i], core_peer)))
        own[i] = partial(place(h, m, core))
        if i >= 1:
            core_stage(i - 1)
        if i == 1:
            z_core.wait_recv()
            z1[...] = z0[...] + zc[...]
            z_mid.append(start(remote(z1, zm, z_send.at[1], z_recv.at[1], mid_peer)))
        if i == 3:
            z_mid[0].wait_recv()
            zh[hi] = z1[...] + zm[...]
            for k in range(nh - 1):
                z_hi.append(
                    start(
                        remote(
                            zh.at[hi], zh.at[hi], z_send.at[2 + k], z_recv.at[2 + k],
                            place(hi_after(k), mid, core),
                        )
                    )
                )
        if i == nh + 2:
            mid_stage(0)
    core_stage(2 * nh - 1)
    for k in range(1, nh):
        mid_stage(k)

    for k in range(nh - 1):
        slot = hi_before(k)
        remote(zh.at[slot], zh.at[slot], z_send.at[2 + k], z_recv.at[2 + k], core_peer).wait_recv()
    z_sum = zh[0]
    for k in range(1, nh):
        z_sum = z_sum + zh[k]
    z_upper, z_lower = split_parts(z_sum[:tokens, :])
    z_t = jnp.transpose(z_sum[:tokens, :])
    t_upper, t_lower = split_parts(z_t)
    sq[0, :, :width] = z_sum[tokens:, :]

    @pl.loop(0, n)
    def _(j):
        x = gat[j]
        grad = mm(t_upper, x) + mm(t_lower, x)
        folded = fold_rows(grad * grad)
        total = folded[:, :width]
        for c0 in range(width, block, width):
            total += folded[:, c0 : c0 + width]
        sq[0, :, :width] += total

    energy = jnp.sum(jnp.sum(sq[0, :, :width], axis=0, keepdims=True), axis=1, keepdims=True)
    entries = depth * width + 2 * rank * cols * n + 2 * cols * n
    inverse = 1.0 / jnp.sqrt(energy / entries + 1e-06)
    mine = tok[...]
    step_a[...] = jnp.transpose((mm(t_upper, mine) + mm(t_lower, mine)) * inverse)
    step_b[...] = step_b[...] * inverse.reshape(1, 1, 1)
    step_m[...] = step_m[...] * inverse
    a_mine = a[rows_of(me), :]
    total = own[2 * nh - 1] + mm_t(z_upper, a_mine) + mm_t(z_lower, a_mine)
    for k in range(nh - 1):
        hi_copies[k].wait_recv()
        total += rh[k].astype(F32)
    gtok[...] = total.astype(BF16)
    for copy in pending:
        copy.wait_send()


def per_device(n, tokens, grad_hidden, w_gate, w_up, a_factors, b_factors, magnitudes):
    count, block = tokens.shape
    depth, cols = w_gate.shape
    width = a_factors.shape[1]
    nh = n // 4
    vmem = pl.BlockSpec(memory_space=pltpu.VMEM)
    hbm = pl.BlockSpec(memory_space=pl.ANY)
    dma = pltpu.SemaphoreType.DMA
    z_shape = (count + 8, width)
    return pl.pallas_call(
        functools.partial(kernel, n),
        out_shape=(
            jax.ShapeDtypeStruct((count, cols), BF16),
            jax.ShapeDtypeStruct((count, block), BF16),
            jax.ShapeDtypeStruct((block, width), F32),
            jax.ShapeDtypeStruct((2, width // 2, cols), F32),
            jax.ShapeDtypeStruct((2, cols), F32),
        ),
        in_specs=[vmem, vmem, hbm, hbm, vmem, vmem, vmem],
        out_specs=(vmem,) * 5,
        scratch_shapes=[
            pltpu.VMEM((2, depth, cols), BF16),
            pltpu.VMEM((n, count, block), BF16),
            pltpu.VMEM((2, width, cols), BF16),
            pltpu.VMEM((2, 8, cols), F32),
            pltpu.VMEM((2, count, cols), F32),
            pltpu.VMEM((count, width), F32),
            pltpu.VMEM((2, count, cols), BF16),
            pltpu.VMEM((2 * nh, count, block), F32),
            pltpu.VMEM((2 * nh, count, block), BF16),
            pltpu.VMEM((2 * nh, count, block), BF16),
            pltpu.VMEM((nh, count, block), BF16),
            pltpu.VMEM((nh, count, block), BF16),
            pltpu.VMEM((nh - 1, count, block), BF16),
            pltpu.VMEM((nh - 1, count, block), BF16),
            pltpu.VMEM(z_shape, F32),
            pltpu.VMEM(z_shape, F32),
            pltpu.VMEM(z_shape, F32),
            pltpu.VMEM(z_shape, F32),
            pltpu.VMEM((nh,) + z_shape, F32),
            dma((2, n)),
            dma((n,)),
            dma((n,)),
            dma((2 * nh,)),
            dma((2 * nh,)),
            dma((nh,)),
            dma((nh,)),
            dma((nh - 1,)),
            dma((nh - 1,)),
            dma((nh + 1,)),
            dma((nh + 1,)),
        ],
        compiler_params=pltpu.CompilerParams(
            collective_id=0, has_side_effects=True, vmem_limit_bytes=60 * 1024 * 1024
        ),
    )(tokens, grad_hidden, w_gate, w_up, a_factors, b_factors, magnitudes)


def solution(mesh):
    in_specs = (
        P("groups", "out"),
        P("groups", "out"),
        P(None, "out"),
        P(None, "out"),
        P(),
        P(None, None, "out"),
        P(None, "out"),
    )
    out_specs = (
        P("groups", "out"),
        P("groups", "out"),
        P(("groups", "out"), None),
        P("groups", None, "out"),
        P("groups", "out"),
    )
    return jax.shard_map(
        functools.partial(per_device, mesh.shape["out"]),
        mesh=mesh, in_specs=in_specs, out_specs=out_specs, check_vma=False,
    )
```

time: 231 us -> 78.6 us (0.34)
  waiting for transfers between devices: 102 us -> 0 us
  Pallas kernels: 0 us -> 69.1 us
  matrix products: 68.7 us -> 0 us
  blocking collectives: 30.5 us -> 0 us
  between operations: 16.6 us -> 0.64 us
  other arithmetic: 7.07 us -> 0 us
  local copies, waits for them, and re-layouts: 5.15 us -> 8.08 us
    reduce_scatter x2 -> x0, waiting for transfers between devices: 72.6 us -> none  [the longest x1 37.7 us: per_device(): lax.psum_scatter(partial_sum, 'out', scatter_dimension=1, tiled=True)]
    pallas_call x0 -> x1, Pallas kernels: none -> 69.1 us  [per_device(): pl.pallas_call(functools.partial(kernel, n), out_shape=(jax.ShapeDtypeStr...]
    dot_general x17 -> x0, matrix products: 68.7 us -> none  [the longest x6 35 us: outer_contract(): lax.dot_general(left_side, right_side, (((1,), (1,)), ((), ())), precisio...]
    psum x1 -> x0, blocking collectives: 30.5 us -> none  [per_device(): energy = lax.psum(local_energy, 'out')]
    all_gather x1 -> x0, waiting for transfers between devices: 28.7 us -> none  [per_device(): whole = lax.all_gather(tokens, 'out', axis=1, tiled=True)]
    reduce_sum x3 -> x0, other arithmetic: 2.97 us -> none  [the longest x1 1.62 us: per_device(): jnp.sum(grad_a * grad_a) + jnp.sum(grad_b * grad_b)]
    unnamed x21 -> x5, local copies, waits for them, and re-layouts: 5.15 us -> 8.08 us
    div x6 -> x0, other arithmetic: 2.47 us -> none  [the longest x1 0.98 us: per_device(): grad_a / rms_value]
  transfers between devices with their start and end apart: 3 -> 0, of which waited for: 3 -> 0; matrix products, arithmetic and copies ran while one was open for 24% -> 0% of each run, Pallas kernels for 0% -> 0%
where the time goes in v2:
time: 78.6 us; the launch traced here: 77.9 us
  Pallas kernels  69.1 us (88%)
  local copies, waits for them, and re-layouts  8.08 us (10%)
    pallas_call x1, Pallas kernels, per_device(): pl.pallas_call(functools.partial(kernel, n), out_shape=(jax.ShapeDtypeStr...  69.1 us
    unnamed x5, local copies, waits for them, and re-layouts  8.08 us

profile of v2, /device:TPU:0, one launch (start us, length us, event | category | flops | bytes accessed | tf_op | source)
XLA Modules:
  0.0 77.9 jit_solution(574114089899365018)
XLA Ops:
  0.6 69.1 %shard_map.110 = (bf16[128,1024]{1,0:T(8,128)(2,1)}, bf16[128,512]{1,0:T(8,128)(2,1)}, f32[512,128]{1,0:T(8,128)}, f32[2,64,1024]{2,1,0:T(8,128)}, f32[2,1024]{1,0:T(2,128)}) custom-call(bf16[128,512]{1,0:T(8,128)(2,1)} %tok.1, bf16[128,1024]{1,0:T(8,128)(2,1)} %gh.1, bf16[8192,1024]{1,0:T(8,128)(2,1)} %wg.1, bf16[8192,1024]{1,0:T(8,128)(2,1)} %wu.1, ...), custom_call_target="tpu_custom_call" | custom-call | tf_op jit(solution)/shard_map/pallas_call | solution.py:328
  69.8 1.7 %copy.17 = bf16[128,1024]{1,0:T(8,128)(2,1)} copy(bf16[128,1024]{1,0:T(8,128)(2,1)} %get-tuple-element.10) | data formatting | bytes 524288
  71.5 1.6 %copy.18 = bf16[128,512]{1,0:T(8,128)(2,1)} copy(bf16[128,512]{1,0:T(8,128)(2,1)} %get-tuple-element.11) | data formatting | bytes 262144
  73.0 1.7 %copy.19 = f32[512,128]{1,0:T(8,128)} copy(f32[512,128]{1,0:T(8,128)} %get-tuple-element.12) | data formatting | bytes 524288
  74.7 1.9 %copy.20 = f32[2,64,1024]{2,1,0:T(8,128)} copy(f32[2,64,1024]{2,1,0:T(8,128)} %get-tuple-element.13) | data formatting | bytes 1048576
  76.6 1.3 %copy.21 = f32[2,1024]{1,0:T(2,128)} copy(f32[2,1024]{1,0:T(2,128)} %get-tuple-element.14) | data formatting | bytes 16384

commit v3 on v2

--- a/solution.py
+++ b/solution.py
@@ -316,6 +316,11 @@
         copy.wait_send()
 
 
+def hand_on(*refs):
+    for source, target in zip(refs[:5], refs[5:]):
+        target[...] = source[...]
+
+
 def per_device(n, tokens, grad_hidden, w_gate, w_up, a_factors, b_factors, magnitudes):
     count, block = tokens.shape
     depth, cols = w_gate.shape
@@ -325,7 +330,7 @@
     hbm = pl.BlockSpec(memory_space=pl.ANY)
     dma = pltpu.SemaphoreType.DMA
     z_shape = (count + 8, width)
-    return pl.pallas_call(
+    results = pl.pallas_call(
         functools.partial(kernel, n),
         out_shape=(
             jax.ShapeDtypeStruct((count, cols), BF16),
@@ -372,6 +377,12 @@
             collective_id=0, has_side_effects=True, vmem_limit_bytes=60 * 1024 * 1024
         ),
     )(tokens, grad_hidden, w_gate, w_up, a_factors, b_factors, magnitudes)
+    return pl.pallas_call(
+        hand_on,
+        out_shape=tuple(jax.ShapeDtypeStruct(r.shape, r.dtype) for r in results),
+        in_specs=[vmem] * 5,
+        out_specs=(vmem,) * 5,
+    )(*results)
 
 
 def solution(mesh):

time: 78.6 us -> 72.7 us (0.925)
  local copies, waits for them, and re-layouts: 8.08 us -> 0 us
  Pallas kernels: 69.1 us -> 71.4 us
    unnamed x5 -> x0, local copies, waits for them, and re-layouts: 8.08 us -> none
    pallas_call x0 -> x1, Pallas kernels: none -> 2.28 us  [per_device(): pl.pallas_call(hand_on, out_shape=tuple((jax.ShapeDtypeStruct(r.shape, r....]
where the time goes in v3:
time: 72.7 us; the launch traced here: 72.1 us
  Pallas kernels  71.4 us (98%)
    pallas_call x1, Pallas kernels, per_device(): pl.pallas_call(functools.partial(kernel, n), out_shape=(jax.ShapeDtypeStr...  69.1 us
    pallas_call x1, Pallas kernels, per_device(): pl.pallas_call(hand_on, out_shape=tuple((jax.ShapeDtypeStruct(r.shape, r....  2.28 us

profile of v3, /device:TPU:0, one launch (start us, length us, event | category | flops | bytes accessed | tf_op | source)
XLA Modules:
  0.0 72.1 jit_solution(3385919455188746922)
XLA Ops:
  0.6 69.1 %shard_map.110 = (bf16[128,1024]{1,0:T(8,128)(2,1)}, bf16[128,512]{1,0:T(8,128)(2,1)}, f32[512,128]{1,0:T(8,128)}, f32[2,64,1024]{2,1,0:T(8,128)}, f32[2,1024]{1,0:T(2,128)}) custom-call(bf16[128,512]{1,0:T(8,128)(2,1)} %tok.1, bf16[128,1024]{1,0:T(8,128)(2,1)} %gh.1, bf16[8192,1024]{1,0:T(8,128)(2,1)} %wg.1, bf16[8192,1024]{1,0:T(8,128)(2,1)} %wu.1, ...), custom_call_target="tpu_custom_call" | custom-call | tf_op jit(solution)/shard_map/pallas_call | solution.py:333
  69.8 2.3 %shard_map.111 = (bf16[128,1024]{1,0:T(8,128)(2,1)}, bf16[128,512]{1,0:T(8,128)(2,1)}, f32[512,128]{1,0:T(8,128)}, f32[2,64,1024]{2,1,0:T(8,128)}, f32[2,1024]{1,0:T(2,128)}) custom-call(bf16[128,1024]{1,0:T(8,128)(2,1)} %get-tuple-element.10.refs_0_, bf16[128,512]{1,0:T(8,128)(2,1)} %get-tuple-element.11.refs_1_, f32[512,128]{1,0:T(8,128)} %get-tuple-element.12.refs_2_, ...), custom_call_target="tpu_custom_call" | custom-call | tf_op jit(solution)/shard_map/pallas_call | solution.py:380
